TPU v7x, 32 devices: a whole 2x2x4 slice. The times are simulated.
32 devices in a mesh: dp: 16 (over z, x, core), tensor: 2 (over y).
Axes of the slice: x: 2, y: 2, z: 4, core: 2. Of those that a mesh axis runs over, the one named last changes fastest.
Arguments:
- inputs: bfloat16 [640, 64, 1024], P('tensor', 'dp'), may hold values from -6 to 6
- pad_mask: int32 [64, 640], P('dp'), may hold values from 0 to 1, as said below
- norm1_gain: bfloat16 [2, 512], P('tensor', 'dp'), may hold values from 0.099609375 to 1.8984375
- norm1_shift: bfloat16 [2, 512], P('tensor', 'dp'), may hold values from -3 to 3
- qkv_weight: bfloat16 [1024, 3, 1024], P('dp', None, 'tensor'), may hold values from -0.1875 to 0.1875
- qv_bias: bfloat16 [2, 2, 512], P(None, 'tensor', 'dp'), may hold values from -3 to 3
- out_weight: bfloat16 [1024, 1024], P('tensor', 'dp'), may hold values from -3 to 3
- out_bias: bfloat16 [2, 512], P('tensor', 'dp'), may hold values from -3 to 3
- norm2_gain: bfloat16 [2, 512], P('tensor', 'dp'), may hold values from 0.099609375 to 1.8984375
- norm2_shift: bfloat16 [2, 512], P('tensor', 'dp'), may hold values from -3 to 3
- up_weight: bfloat16 [1024, 4096], P('dp', 'tensor'), may hold values from -0.1875 to 0.1875
- up_bias: bfloat16 [2, 2048], P('tensor', 'dp'), may hold values from -3 to 3
- down_weight: bfloat16 [4096, 1024], P('tensor', 'dp'), may hold values from -0.09375 to 0.09375
- down_bias: bfloat16 [2, 512], P('tensor', 'dp'), may hold values from -3 to 3
- cotangent: float32 [640, 64, 1024], P('tensor', 'dp'), may hold values from -6 to 6
Outputs:
- block_output: float32 [640, 64, 1024], P('tensor', 'dp')
- input_grad: float32 [640, 64, 1024], P('tensor', 'dp')
- gain_one_grad: float32 [2, 512], P('tensor', 'dp')
- shift_one_grad: float32 [2, 512], P('tensor', 'dp')
- qkv_weight_grad: float32 [1024, 3, 1024], P('dp', None, 'tensor')
- qv_bias_grad: float32 [2, 2, 512], P(None, 'tensor', 'dp')
- out_weight_grad: float32 [1024, 1024], P('tensor', 'dp')
- out_bias_grad: float32 [2, 512], P('tensor', 'dp')
- gain_two_grad: float32 [2, 512], P('tensor', 'dp')
- shift_two_grad: float32 [2, 512], P('tensor', 'dp')
- up_weight_grad: float32 [1024, 4096], P('dp', 'tensor')
- up_bias_grad: float32 [2, 2048], P('tensor', 'dp')
- down_weight_grad: float32 [4096, 1024], P('tensor', 'dp')
- down_bias_grad: float32 [2, 512], P('tensor', 'dp')
Inputs may be any that keep to these rules, and one draw needn't show every extreme that they name: `pad_mask`: each image's row holds ones on its first slots and zeros after them; it has between 289 and 577 ones, and image 0 has exactly 577.
All inputs are finite; a program needn't handle non-finite values.
Results may differ from a plain program's by a relative error of at most 0.0085.
The roundings to bfloat16 on the way count: a program that leaves them out, or rounds other values in their place, can miss the bound.
Values may be sent and summed in bfloat16 or wider, within the bound.
No kernel may reach another device: no remote copies, remote signals or barrier semaphores. Data moves between devices by JAX's collectives and lax.ppermute only.
A program may use at most 256 MiB of HBM per device.

v0:
```python
import jax
import jax.numpy as jnp
from jax import lax
from jax.sharding import PartitionSpec as P

HD = 64
epsilon = 1e-06
masked_score = -1e30


def layer_norm(values, gain, shift):
    row_mean = jnp.mean(values, axis=-1, keepdims=True)
    centred = values - row_mean
    spread = jnp.mean(centred * centred, axis=-1, keepdims=True)
    return centred * lax.rsqrt(spread + epsilon) * gain + shift


def gelu_exact(values):
    return jax.nn.gelu(values, approximate=False)


def image_scores(queries, key_rows, kept_row):
    scores = jnp.einsum(
        "qhe,khe->hqk", queries, key_rows, preferred_element_type=jnp.float32
    ) * HD ** (-0.5)
    return jnp.where(kept_row[None, None, :], scores, masked_score)


def forward_image(operands):
    queries, key_rows, value_rows, kept_row = operands
    scores = image_scores(queries, key_rows, kept_row)
    row_max = jnp.max(scores, axis=-1, keepdims=True)
    exps = jnp.exp(scores - row_max)
    row_total = jnp.sum(exps, axis=-1, keepdims=True)
    soft_weights = (exps / row_total).astype(jnp.bfloat16)
    attended = jnp.einsum(
        "hqk,khe->qhe", soft_weights, value_rows, preferred_element_type=jnp.float32
    )
    return (attended.astype(jnp.bfloat16), (row_max + jnp.log(row_total))[..., 0])


def backward_image(operands):
    queries, key_rows, value_rows, kept_row, log_total, attended_grad = operands
    seq_length = queries.shape[0]
    scores = image_scores(queries, key_rows, kept_row)
    soft_float = jnp.exp(scores - log_total[..., None])
    soft_weights = soft_float.astype(jnp.bfloat16)
    value_grad = jnp.einsum(
        "hqk,qhe->khe", soft_weights, attended_grad, preferred_element_type=jnp.float32
    )
    prob_grad = jnp.einsum(
        "qhe,khe->hqk", attended_grad, value_rows, preferred_element_type=jnp.float32
    )
    score_grad = soft_float * (prob_grad - jnp.sum(prob_grad * soft_float, axis=-1, keepdims=True))
    score_grad = score_grad.astype(jnp.bfloat16)
    query_grad = jnp.einsum(
        "hqk,khe->qhe", score_grad, key_rows, preferred_element_type=jnp.float32
    ) * HD ** (-0.5)
    key_grad = jnp.einsum(
        "hqk,qhe->khe", score_grad, queries, preferred_element_type=jnp.float32
    ) * HD ** (-0.5)
    joined = jnp.concatenate(
        [
            query_grad.reshape(seq_length, -1),
            key_grad.reshape(seq_length, -1),
            value_grad.reshape(seq_length, -1),
        ],
        axis=-1,
    )
    return joined.astype(jnp.bfloat16)


def on_device(
    inputs,
    pad_mask,
    norm1_gain,
    norm1_shift,
    qkv_weight,
    qv_bias,
    out_weight,
    out_bias,
    norm2_gain,
    norm2_shift,
    up_weight,
    up_bias,
    down_weight,
    down_bias,
    cotangent,
):
    local_rows = inputs.shape[0]
    image_count = inputs.shape[1]
    model_width = inputs.shape[2]
    seq_length = pad_mask.shape[1]
    tensor_count = lax.axis_size("tensor")
    vector_stack = jnp.stack(
        [norm1_gain, norm1_shift, out_bias, norm2_gain, norm2_shift, down_bias], axis=0
    )
    gathered = (
        lax.all_gather(qkv_weight, "dp", axis=0, tiled=True),
        lax.all_gather(out_weight, "dp", axis=1, tiled=True),
        lax.all_gather(up_weight, "dp", axis=0, tiled=True),
        lax.all_gather(down_weight, "dp", axis=1, tiled=True),
        lax.all_gather(qv_bias, "dp", axis=2, tiled=True),
        lax.all_gather(up_bias, "dp", axis=1, tiled=True),
        lax.all_gather(vector_stack, "dp", axis=2, tiled=True),
    )
    qkv_full, out_full, up_full, down_full, bias_pair, bias_hidden, vector_part = gathered
    local_width = qkv_full.shape[2]
    head_count = local_width // HD
    vector_rows = (
        lax.all_gather(vector_part, "tensor", axis=1, tiled=True)
        .reshape(6, model_width)
        .astype(jnp.float32)
    )
    gain_one, shift_one, out_shift, gain_two, shift_two, down_shift = [
        vector_rows[index] for index in range(6)
    ]
    qkv_matrix = qkv_full.reshape(model_width, 3 * local_width)
    bias_row = jnp.concatenate(
        [
            bias_pair[0, 0].astype(jnp.float32),
            jnp.zeros((local_width,), jnp.float32),
            bias_pair[1, 0].astype(jnp.float32),
        ]
    )
    up_row = bias_hidden.reshape(-1).astype(jnp.float32)
    kept_all = pad_mask > 0
    first_row = lax.axis_index("tensor") * local_rows
    kept_float = jnp.transpose(lax.dynamic_slice_in_dim(kept_all, first_row, local_rows, 1)).astype(
        jnp.float32
    )[:, :, None]
    input_float = inputs.astype(jnp.float32)
    normed_one = layer_norm(input_float, gain_one, shift_one).astype(jnp.bfloat16)
    normed_all = lax.all_gather(normed_one, "tensor", axis=0, tiled=True)
    qkv_rows = (
        jnp.einsum("sbd,dc->sbc", normed_all, qkv_matrix, preferred_element_type=jnp.float32)
        + bias_row
    )
    qkv_rows = qkv_rows.astype(jnp.bfloat16)
    qkv_images = jnp.swapaxes(qkv_rows, 0, 1).reshape(image_count, seq_length, 3, head_count, HD)
    query_all = qkv_images[:, :, 0]
    key_all = qkv_images[:, :, 1]
    value_all = qkv_images[:, :, 2]
    attended_img, log_totals = lax.map(forward_image, (query_all, key_all, value_all, kept_all))
    attended_rows = jnp.swapaxes(attended_img.reshape(image_count, seq_length, local_width), 0, 1)
    row_block = attended_rows
    projected = lax.psum_scatter(
        jnp.einsum("sbc,cd->sbd", row_block, out_full, preferred_element_type=jnp.float32),
        "tensor",
        scatter_dimension=0,
        tiled=True,
    )
    after_attn = input_float + projected + out_shift
    normed_two = layer_norm(after_attn, gain_two, shift_two).astype(jnp.bfloat16)
    normed_all_two = lax.all_gather(normed_two, "tensor", axis=0, tiled=True)
    up_values = (
        jnp.einsum("sbd,df->sbf", normed_all_two, up_full, preferred_element_type=jnp.float32)
        + up_row
    )
    activated = gelu_exact(up_values).astype(jnp.bfloat16)
    row_block = activated
    mlp_out = lax.psum_scatter(
        jnp.einsum("sbf,fd->sbd", row_block, down_full, preferred_element_type=jnp.float32),
        "tensor",
        scatter_dimension=0,
        tiled=True,
    )
    block_output = (after_attn + mlp_out + down_shift) * kept_float
    qkv_back, out_back, up_back, down_back = (qkv_matrix, out_full, up_full, down_full)
    out_grad = cotangent * kept_float
    down_shift_grad = jnp.sum(out_grad, axis=(0, 1))
    out_low = out_grad.astype(jnp.bfloat16)
    out_low_all = lax.all_gather(out_low, "tensor", axis=0, tiled=True)
    down_weight_grad = jnp.einsum(
        "sbf,sbd->fd", activated, out_low_all, preferred_element_type=jnp.float32
    )
    act_grad = jnp.einsum("sbd,fd->sbf", out_low_all, down_back, preferred_element_type=jnp.float32)
    _, gelu_back = jax.vjp(gelu_exact, up_values)
    up_grad = gelu_back(act_grad)[0].astype(jnp.bfloat16)
    up_shift_grad = jnp.sum(up_grad.astype(jnp.float32), axis=(0, 1))
    up_weight_grad = jnp.einsum(
        "sbd,sbf->df", normed_all_two, up_grad, preferred_element_type=jnp.float32
    )
    row_block = up_grad
    normed_two_grad = lax.psum_scatter(
        jnp.einsum("sbf,df->sbd", row_block, up_back, preferred_element_type=jnp.float32),
        "tensor",
        scatter_dimension=0,
        tiled=True,
    )
    _, norm_two_back = jax.vjp(layer_norm, after_attn, gain_two, shift_two)
    attn_side, gain_two_grad, shift_two_grad = norm_two_back(normed_two_grad)
    after_attn_grad = out_grad + attn_side
    out_shift_grad = jnp.sum(after_attn_grad, axis=(0, 1))
    proj_low = after_attn_grad.astype(jnp.bfloat16)
    proj_low_all = lax.all_gather(proj_low, "tensor", axis=0, tiled=True)
    out_weight_grad = jnp.einsum(
        "sbc,sbd->cd", attended_rows, proj_low_all, preferred_element_type=jnp.float32
    )
    attended_grad = jnp.einsum(
        "sbd,cd->sbc", proj_low_all, out_back, preferred_element_type=jnp.float32
    )
    attended_grad = attended_grad.astype(jnp.bfloat16)
    attended_grad_img = jnp.swapaxes(attended_grad, 0, 1).reshape(
        image_count, seq_length, head_count, HD
    )
    qkv_grad_img = lax.map(
        backward_image, (query_all, key_all, value_all, kept_all, log_totals, attended_grad_img)
    )
    qkv_grad = jnp.swapaxes(qkv_grad_img, 0, 1)
    qkv_sums = jnp.sum(qkv_grad.astype(jnp.float32), axis=(0, 1))
    qv_grad = jnp.stack([qkv_sums[:local_width], qkv_sums[2 * local_width :]], axis=0).reshape(
        2, 1, local_width
    )
    qkv_weight_grad = jnp.einsum(
        "sbd,sbc->dc", normed_all, qkv_grad, preferred_element_type=jnp.float32
    )
    qkv_weight_grad = qkv_weight_grad.reshape(model_width, 3, local_width)
    row_block = qkv_grad
    normed_one_grad = lax.psum_scatter(
        jnp.einsum("sbc,dc->sbd", row_block, qkv_back, preferred_element_type=jnp.float32),
        "tensor",
        scatter_dimension=0,
        tiled=True,
    )
    _, norm_one_back = jax.vjp(layer_norm, input_float, gain_one, shift_one)
    input_side, gain_one_grad, shift_one_grad = norm_one_back(normed_one_grad)
    input_grad = after_attn_grad + input_side
    vector_grads = jnp.stack(
        [
            gain_one_grad,
            shift_one_grad,
            out_shift_grad,
            gain_two_grad,
            shift_two_grad,
            down_shift_grad,
        ],
        axis=0,
    ).reshape(6, tensor_count, model_width // tensor_count)
    vector_local = lax.psum_scatter(vector_grads, "tensor", scatter_dimension=1, tiled=True)
    owned = (
        lax.psum_scatter(qkv_weight_grad, "dp", scatter_dimension=0, tiled=True),
        lax.psum_scatter(out_weight_grad, "dp", scatter_dimension=1, tiled=True),
        lax.psum_scatter(up_weight_grad, "dp", scatter_dimension=0, tiled=True),
        lax.psum_scatter(down_weight_grad, "dp", scatter_dimension=1, tiled=True),
        lax.psum_scatter(qv_grad, "dp", scatter_dimension=2, tiled=True),
        lax.psum_scatter(up_shift_grad.reshape(1, -1), "dp", scatter_dimension=1, tiled=True),
        lax.psum_scatter(vector_local, "dp", scatter_dimension=2, tiled=True),
    )
    qkv_owned, out_owned, up_owned, down_owned, qv_owned, hidden_owned, vector_owned = owned
    return (
        block_output,
        input_grad,
        vector_owned[0],
        vector_owned[1],
        qkv_owned,
        qv_owned,
        out_owned,
        vector_owned[2],
        vector_owned[3],
        vector_owned[4],
        up_owned,
        hidden_owned,
        down_owned,
        vector_owned[5],
    )


def solution(mesh):
    in_specs = (
        P("tensor", "dp", None),
        P("dp", None),
        P("tensor", "dp"),
        P("tensor", "dp"),
        P("dp", None, "tensor"),
        P(None, "tensor", "dp"),
        P("tensor", "dp"),
        P("tensor", "dp"),
        P("tensor", "dp"),
        P("tensor", "dp"),
        P("dp", "tensor"),
        P("tensor", "dp"),
        P("tensor", "dp"),
        P("tensor", "dp"),
        P("tensor", "dp", None),
    )
    out_specs = (
        P("tensor", "dp", None),
        P("tensor", "dp", None),
        P("tensor", "dp"),
        P("tensor", "dp"),
        P("dp", None, "tensor"),
        P(None, "tensor", "dp"),
        P("tensor", "dp"),
        P("tensor", "dp"),
        P("tensor", "dp"),
        P("tensor", "dp"),
        P("dp", "tensor"),
        P("tensor", "dp"),
        P("tensor", "dp"),
        P("tensor", "dp"),
    )
    return jax.shard_map(
        on_device, mesh=mesh, in_specs=in_specs, out_specs=out_specs, check_vma=False
    )
```

profile of v0, /device:TPU:0, one launch (start us, length us, event | category | flops | bytes accessed | tf_op | source)
XLA Modules:
  0.0 1860.6 jit_solution(15390352596484088534)
XLA Ops:
  12.1 23.8 %all_gather.36 = bf16[6,1,512]{0,1,2:T(2,128)(2,1)S(1)} all-gather(bf16[6,1,32]{0,1,2:T(2,128)(2,1)S(1)} %copy.88), channel_id=1, replica_groups=mesh['dp'=16,'tensor'=2] {'dp'}, dimensions={2}, use_global_device_ids=true | all-gather | bytes 6528 | tf_op jit(solution)/shard_map/all_gather | solution.py:105
  36.0 4.4 all_gather.37
  49.8 18.0 all_gather.40
  73.5 54.6 %all-gather.9.cloned.1.call-done = bf16[640,4,1024]{2,0,1:T(8,128)(2,1)} async-done(((bf16[320,4,1024]{2,0,1:T(8,128)(2,1)}), bf16[640,4,1024]{2,0,1:T(8,128)(2,1)}) %all-gather.9.cloned.1.call-update) | async-done | bytes 5242896 | tf_op jit(solution)/shard_map/all_gather | solution.py:134
  128.1 12.9 fusion.50
  141.0 10.6 copy.93
  151.6 5.4 slice_bitcast_fusion
  157.0 51.5 %while.22 = (s32[]{:T(128)}, bf16[4,640,8,64]{1,3,2,0:T(8,128)(2,1)}, f32[4,8,640]{2,1,0:T(8,128)}, bf16[4,640,8,64]{1,3,2,0:T(8,128)(2,1)}, pred[4,640]{1,0:T(4...) while((s32[]{:T(128)}, ...), condition=%wide.region_5.6_spmd, body=%wide.region_2.5_spmd.sunk | while | flops 878504960 | bytes 42113112 | solution.py:144
  164.5 5.6 fusion.136
  177.3 5.5 fusion.136
  190.2 5.5 fusion.136
  203.0 5.5 fusion.136
  208.6 4.9 copy.94
  213.5 8.9 fusion.80
  223.5 120.9 %reduce-scatter.18.cloned.1.call-done = f32[320,4,1024]{2,0,1:T(8,128)} async-done(((f32[640,4,1024]{2,0,1:T(8,128)}), f32[320,4,1024]{2,0,1:T(8,128)}) %reduce-scatter.18.cloned.1.call-update) | async-done | bytes 5242896 | tf_op jit(solution)/shard_map/reduce_scatter | solution.py:147
  353.2 7.3 fusion.77
  361.3 21.3 %all_gather.44 = bf16[1,2048]{1,0:T(2,128)(2,1)S(1)} all-gather(bf16[1,128]{1,0:T(2,128)(2,1)S(1)} %copy-done.29), channel_id=1, replica_groups=mesh['dp'=16,'tensor'=2] {'dp'}, dimensions={1}, use_global_device_ids=true | all-gather | bytes 4352 | tf_op jit(solution)/shard_map/all_gather | solution.py:104
  382.7 14.3 all-gather.17.cloned.1.call-done
  397.0 68.5 %all-gather.15.cloned.1.call-done = bf16[640,4,1024]{2,0,1:T(8,128)(2,1)} async-done(((bf16[320,4,1024]{2,0,1:T(8,128)(2,1)}), bf16[640,4,1024]{2,0,1:T(8,128)(2,1)}) %all-gather.15.cloned.1.call-update) | async-done | bytes 5242896 | tf_op jit(solution)/shard_map/all_gather | solution.py:155
  465.5 24.9 %fusion.68 = (u8[640,2048]{1,0:T(8,128)(4,1)S(1)}, u8[640,2048]{1,0:T(8,128)(4,1)S(1)}, f32[640,4,2048]{2,0,1:T(8,128)}) fusion(f32[2048]{0:T(1024)S(1)} %bitcast.227, bf16[640,4,1024]{2,0,1:T(8,128)(2,1)} %all-gather.15.cloned.1.call-done, bf16[1024,2048]{1,0:T(8,128)(2,1)} %all-gather.17.cloned.1.call-done), kind=kOutput, calls=%fused_computation.110 | convolution fusion | flops 10808197120 | bytes 33038336 | tf_op jit(solution)/shard_map/sbd,df->sbf/dot_general | solution.py:157
  490.4 51.1 %multiply_convert_fusion.1 = (bf16[640,4,2048]{2,0,1:T(8,128)(2,1)}, f32[640,4,2048]{2,0,1:T(8,128)}) fusion(f32[640,4,2048]{2,0,1:T(8,128)} %get-tuple-element.224, f32[2048]{0:T(1024)S(1)} %bitcast.228, u8[640,2048]{1,0:T(8,128)(4,1)S(1)} %get-tuple-element.154, u8[640,2048]{1,0:T(8,128)(4,1)S(1)} %get-tuple-element.153), kind=kLoop, calls=%fused_computation.64 | loop fusion | flops 372244480 | bytes 55058432 | tf_op jit(solution)/shard_map/convert_element_type | solution.py:160
  541.5 46.9 %all-gather.19.cloned.1.call-done = bf16[2048,1024]{0,1:T(8,128)(2,1)} async-done(((bf16[2048,64]{0,1:T(8,128)(2,1)}), bf16[2048,1024]{0,1:T(8,128)(2,1)}) %all-gather.19.cloned.1.call-update) | async-done | bytes 4194320 | tf_op jit(solution)/shard_map/all_gather | solution.py:102
  588.4 27.9 %convert_reduce_fusion = (f32[2048]{0:T(1024)}, bf16[640,4,2048]{2,0,1:T(8,128)(2,1)}) fusion(f32[640,4,2048]{2,0,1:T(8,128)} %get-tuple-element.198, bf16[640,4,1024]{2,0,1:T(8,128)(2,1)} %all-gather.21.cloned.1.call-done, bf16[2048,1024]{0,1:T(8,128)(2,1)} %all-gather.19.cloned.1.call-done, f32[640,4,2048]{2,0,1:T(8,128)} %get-tuple-element.224, ...), kind=kOutput, calls=%fused_computation.62 | convolution fusion | flops 10826545152 | bytes 61882368 | tf_op jit(solution)/shard_map/sbd,fd->sbf/dot_general | solution.py:177
  616.3 17.4 fusion.72
  633.8 17.5 fusion.70
  651.4 102.8 %reduce-scatter.22.cloned.1.call-done = f32[320,4,1024]{2,0,1:T(8,128)} async-done(((f32[640,4,1024]{2,0,1:T(8,128)}), f32[320,4,1024]{2,0,1:T(8,128)}) %reduce-scatter.22.cloned.1.call-update) | async-done | bytes 5242896 | tf_op jit(solution)/shard_map/reduce_scatter | solution.py:185
  754.2 6.0 fusion.93
  760.2 4.8 multiply_reduce_fusion.1
  765.0 113.3 %reduce-scatter.20.cloned.1.call-done = f32[320,4,1024]{2,0,1:T(8,128)} async-done(((f32[640,4,1024]{2,0,1:T(8,128)}), f32[320,4,1024]{2,0,1:T(8,128)}) %reduce-scatter.20.cloned.1.call-update) | async-done | bytes 5242896 | tf_op jit(solution)/shard_map/reduce_scatter | solution.py:162
  878.3 11.7 fusion.95
  894.7 68.3 %all-gather.23.cloned.1.call-done = bf16[640,4,1024]{2,0,1:T(8,128)(2,1)} async-done(((bf16[320,4,1024]{2,0,1:T(8,128)(2,1)}), bf16[640,4,1024]{2,0,1:T(8,128)(2,1)}) %all-gather.23.cloned.1.call-update) | async-done | bytes 5242896 | tf_op jit(solution)/shard_map/all_gather | solution.py:196
  962.9 7.2 convolution_convert_fusion
  970.2 113.1 %while.23 = (s32[]{:T(128)}, bf16[4,640,1536]{1,2,0:T(8,128)(2,1)}, bf16[4,640,8,64]{1,3,2,0:T(8,128)(2,1)S(1)}, pred[4,640]{1,0:T(4,128)(4,1)S(1)}, bf16[4,640,...) while((s32[]{:T(128)}, bf16[4,640,1536]{1,2,0:T(8,128)(2,1)}, ...), condition=%wide.region_15.16_spmd, body=%wide.region_13.15_spmd.sunk | while | flops 2134174720 | bytes 108898144 | solution.py:207
  970.9 4.5 subtract_exponential_fusion.3
  975.4 7.9 multiply_reduce_fusion.5
  983.3 5.9 multiply_convert_fusion.3
  999.2 4.5 subtract_exponential_fusion.3
  1003.7 7.9 multiply_reduce_fusion.5
  1011.6 5.9 multiply_convert_fusion.3
  1027.5 4.5 subtract_exponential_fusion.3
  1032.0 7.9 multiply_reduce_fusion.5
  1039.8 5.9 multiply_convert_fusion.3
  1055.8 4.5 subtract_exponential_fusion.3
  1060.3 7.9 multiply_reduce_fusion.5
  1068.1 5.9 multiply_convert_fusion.3
  1083.3 14.2 fusion.53
  1099.6 4.3 convert_reduce_fusion.1
  1105.6 13.3 fusion.51
  1118.9 9.6 copy.100
  1129.8 89.7 %reduce-scatter.24.cloned.1.call-done = f32[320,4,1024]{2,0,1:T(8,128)} async-done(((f32[640,4,1024]{2,0,1:T(8,128)}), f32[320,4,1024]{2,0,1:T(8,128)}) %reduce-scatter.24.cloned.1.call-update) | async-done | bytes 5242896 | tf_op jit(solution)/shard_map/reduce_scatter | solution.py:220
  1219.5 4.4 fusion.94
  1227.6 7.3 all-reduce
  1240.5 17.4 convolution_bitcast_fusion.1
  1258.0 17.5 convolution_bitcast_fusion
  1275.8 7.6 fusion.83
  1286.1 8.2 copy.101
  1294.4 44.9 %reduce-scatter.34.cloned.1.call-done = f32[32,2]{1,0:T(8,128)} async-done(((f32[512,2]{1,0:T(8,128)}), f32[32,2]{1,0:T(8,128)}) %reduce-scatter.34.cloned.1.call-update) | async-done | bytes 272
  1340.7 171.6 %all-reduce.4.cloned.1.call-done = f32[1024,3,512]{2,1,0:T(4,128)} async-done(((f32[1024,3,512]{2,1,0:T(4,128)}), f32[1024,3,512]{2,1,0:T(4,128)}) %all-reduce.4.cloned.1.call-update) | async-done | bytes 6291472
  1514.3 5.3 add_add_fusion.2
  1519.6 5.7 copy.102
  1525.3 45.6 %reduce-scatter.32.cloned.1.call-done = f32[32,6]{1,0:T(8,128)} async-done(((f32[512,6]{1,0:T(8,128)}), f32[32,6]{1,0:T(8,128)}) %reduce-scatter.32.cloned.1.call-update) | async-done | bytes 784
  1575.3 103.8 %reduce-scatter.28.cloned.1.call-done = f32[64,2048]{1,0:T(8,128)} async-done(((f32[1024,2048]{1,0:T(8,128)}), f32[64,2048]{1,0:T(8,128)}) %reduce-scatter.28.cloned.1.call-update) | async-done | bytes 524304 | tf_op jit(solution)/shard_map/reduce_scatter | solution.py:244
  1679.0 108.9 %reduce-scatter.30.cloned.1.call-done = f32[2048,64]{0,1:T(8,128)} async-done(((f32[2048,1024]{0,1:T(8,128)}), f32[2048,64]{0,1:T(8,128)}) %reduce-scatter.30.cloned.1.call-update) | async-done | bytes 524304 | tf_op jit(solution)/shard_map/reduce_scatter | solution.py:245
  1788.0 65.7 %reduce-scatter.26.cloned.1.call-done = f32[512,64]{0,1:T(8,128)} async-done(((f32[512,1024]{0,1:T(8,128)}), f32[512,64]{0,1:T(8,128)}) %reduce-scatter.26.cloned.1.call-update) | async-done | bytes 131088 | tf_op jit(solution)/shard_map/reduce_scatter | solution.py:243
  (218 shorter events, 128.9 us)
Async XLA Ops:
  7.2 36.4 %copy-start.1 = (bf16[320,4,1024]{2,1,0:T(4,128)(2,1)S(1)}, bf16[320,4,1024]{2,1,0:T(4,128)(2,1)}, u32[]{:S(2)}) copy-start(bf16[320,4,1024]{2,1,0:T(4,128)(2,1)} %param.19) | copy-start | bytes 7864324
  7.2 63.0 %all-gather.11.cloned.1.call-start = ((), (), s32[]{:S(2)}) async-start(), calls=%async_computation.11 | async-start | bytes 3342336 | tf_op jit(solution)/shard_map/all_gather | solution.py:99
  7.9 120.2 %all-gather.9.cloned.1.call-start = ((), (), s32[]{:S(2)}) async-start(), calls=%async_computation.10 | async-start | bytes 7864320 | tf_op jit(solution)/shard_map/all_gather | solution.py:134
  43.6 2.2 copy-start.10
  43.6 6.1 copy-start.28
  43.6 26.5 %copy-start.26 = (s32[4,640]{1,0:T(4,128)S(1)}, s32[4,640]{1,0:T(4,128)}, u32[]{:S(2)}) copy-start(s32[4,640]{1,0:T(4,128)} %param.20) | copy-start | bytes 30724
  45.1 0.7 copy-start.17
  45.2 0.6 copy-start.15
  45.8 0.6 copy-start.13
  48.9 164.6 %all-gather.13.cloned.1.call-start = ((), (), s32[]{:S(2)}) async-start(), calls=%async_computation.12 | async-start | bytes 1114112 | tf_op jit(solution)/shard_map/all_gather | solution.py:100
  49.6 294.8 %reduce-scatter.18.cloned.1.call-start = ((), (), s32[]{:S(2)}) async-start(), calls=%async_computation.13 | async-start | bytes 15728640 | tf_op jit(solution)/shard_map/reduce_scatter | solution.py:147
  73.5 67.5 %copy-start.9 = (bf16[1024,3,512]{0,2,1:T(8,128)(2,1)}, bf16[1024,3,512]{0,2,1:T(8,128)(2,1)S(1)}, u32[]{:S(2)}) copy-start(bf16[1024,3,512]{0,2,1:T(8,128)(2,1)S(1)} %copy.90) | copy-start | bytes 9437188
  208.6 13.9 copy-start.7
  222.4 122.0 %copy-start.2 = (bf16[320,4,1024]{2,1,0:T(4,128)(2,1)S(1)}, bf16[320,4,1024]{2,1,0:T(4,128)(2,1)}, u32[]{:S(2)}) copy-start(bf16[320,4,1024]{2,1,0:T(4,128)(2,1)} %param.19) | copy-start | bytes 7864324
  222.4 122.0 %copy-start.22 = (f32[1,2,512]{2,0,1:T(1,128)S(1)}, f32[1,2,512]{2,0,1:T(1,128)}, u32[]{:S(2)}) copy-start(f32[1,2,512]{2,0,1:T(1,128)} %get-tuple-element.219) | copy-start | bytes 12292
  222.4 174.6 %all-gather.17.cloned.1.call-start = ((), (), s32[]{:S(2)}) async-start(), calls=%async_computation.15 | async-start | bytes 4456448 | tf_op jit(solution)/shard_map/all_gather | solution.py:101
  223.0 242.5 %all-gather.15.cloned.1.call-start = ((), (), s32[]{:S(2)}) async-start(), calls=%async_computation.14 | async-start | bytes 7864320 | tf_op jit(solution)/shard_map/all_gather | solution.py:155
  348.6 2.4 copy-start
  348.6 2.4 copy-start.12
  348.6 2.3 copy-start.19
  353.0 188.5 %all-gather.21.cloned.1.call-start = ((), (), s32[]{:S(2)}) async-start(), calls=%async_computation.18 | async-start | bytes 7864320 | tf_op jit(solution)/shard_map/all_gather | solution.py:173
  353.2 8.2 copy-start.29
  360.5 227.9 %all-gather.19.cloned.1.call-start = ((), (), s32[]{:S(2)}) async-start(), calls=%async_computation.16 | async-start | bytes 4456448 | tf_op jit(solution)/shard_map/all_gather | solution.py:102
  361.3 392.9 %reduce-scatter.22.cloned.1.call-start = ((), (), s32[]{:S(2)}) async-start(), calls=%async_computation.19 | async-start | bytes 15728640 | tf_op jit(solution)/shard_map/reduce_scatter | solution.py:185
  633.7 244.5 %reduce-scatter.20.cloned.1.call-start = ((), (), s32[]{:S(2)}) async-start(), calls=%async_computation.17 | async-start | bytes 15728640 | tf_op jit(solution)/shard_map/reduce_scatter | solution.py:162
  651.3 311.6 %all-gather.23.cloned.1.call-start = ((), (), s32[]{:S(2)}) async-start(), calls=%async_computation.20 | async-start | bytes 7864320 | tf_op jit(solution)/shard_map/all_gather | solution.py:196
  754.2 6.0 copy-start.4
  760.2 118.1 %copy-start.21 = (f32[1,2,512]{2,0,1:T(1,128)S(1)}, f32[1,2,512]{2,0,1:T(1,128)}, u32[]{:S(2)}) copy-start(f32[1,2,512]{2,0,1:T(1,128)} %get-tuple-element.216) | copy-start | bytes 12292
  889.9 2.3 copy-start.6
  894.2 325.3 %reduce-scatter.24.cloned.1.call-start = ((), (), s32[]{:S(2)}) async-start(), calls=%async_computation.21 | async-start | bytes 15728640 | tf_op jit(solution)/shard_map/reduce_scatter | solution.py:220
  894.7 75.5 %copy-start.8 = (bf16[4,640,8,64]{1,3,2,0:T(8,128)(2,1)S(1)}, bf16[4,640,8,64]{1,3,2,0:T(8,128)(2,1)}, u32[]{:S(2)}) copy-start(bf16[4,640,8,64]{1,3,2,0:T(8,128)(2,1)} %copy-done.7) | copy-start | bytes 7864324
  1097.5 0.7 copy-start.27
  1097.5 187.2 %reduce-scatter.36.cloned.1.call-start = ((), (), s32[]{:S(2)}) async-start(), calls=%async_computation.27 | async-start | bytes 1114112
  1099.5 239.7 %reduce-scatter.34.cloned.1.call-start = ((), (), s32[]{:S(2)}) async-start(), calls=%async_computation.26 | async-start | bytes 278528
  1105.6 406.7 %all-reduce.4.cloned.1.call-start = ((), (), s32[]{:S(2)}) async-start(), calls=%async_computation.28 | async-start | bytes 16777216
  1128.5 0.7 copy-start.31
  1128.5 1.2 copy-start.25
  1128.5 1.2 copy-start.20
  1128.5 1.3 copy-start.23
  1128.5 1.3 copy-start.24
  1128.5 91.0 %copy-start.3 = (bf16[320,4,1024]{2,1,0:T(4,128)(2,1)S(1)}, bf16[320,4,1024]{2,1,0:T(4,128)(2,1)}, u32[]{:S(2)}) copy-start(bf16[320,4,1024]{2,1,0:T(4,128)(2,1)} %param.19) | copy-start | bytes 7864324
  1128.5 91.0 %copy-start.11 = (f32[320,4]{0,1:T(4,128)S(1)}, f32[320,4]{0,1:T(4,128)}, u32[]{:S(2)}) copy-start(f32[320,4]{0,1:T(4,128)} %copy-done.10) | copy-start | bytes 15364
  1128.5 91.0 %copy-start.14 = (f32[1,2,512]{2,0,1:T(1,128)S(1)}, f32[1,2,512]{2,0,1:T(1,128)}, u32[]{:S(2)}) copy-start(f32[1,2,512]{2,0,1:T(1,128)} %copy-done.13) | copy-start | bytes 12292
  1128.6 95.3 %copy-start.18 = (f32[320,4]{0,1:T(4,128)S(1)}, f32[320,4]{0,1:T(4,128)}, u32[]{:S(2)}) copy-start(f32[320,4]{0,1:T(4,128)} %copy-done.17) | copy-start | bytes 15364
  1128.6 95.4 %copy-start.16 = (f32[320,4]{0,1:T(4,128)S(1)}, f32[320,4]{0,1:T(4,128)}, u32[]{:S(2)}) copy-start(f32[320,4]{0,1:T(4,128)} %copy-done.15) | copy-start | bytes 15364
  1128.6 442.3 %reduce-scatter.32.cloned.1.call-start = ((), (), s32[]{:S(2)}) async-start(), calls=%async_computation.25 | async-start | bytes 278528
  1219.5 4.5 copy-start.5
  1240.5 438.5 %reduce-scatter.28.cloned.1.call-start = ((), (), s32[]{:S(2)}) async-start(), calls=%async_computation.23 | async-start | bytes 8912896 | tf_op jit(solution)/shard_map/reduce_scatter | solution.py:244
  1258.0 530.0 %reduce-scatter.30.cloned.1.call-start = ((), (), s32[]{:S(2)}) async-start(), calls=%async_computation.24 | async-start | bytes 8912896 | tf_op jit(solution)/shard_map/reduce_scatter | solution.py:245
  1275.5 8.0 copy-start.30
  1275.5 578.1 %reduce-scatter.26.cloned.1.call-start = ((), (), s32[]{:S(2)}) async-start(), calls=%async_computation.22 | async-start | bytes 2228224 | tf_op jit(solution)/shard_map/reduce_scatter | solution.py:243
Sparse Core Ops, SparseCore 0:
  10.2 48.9 all-gather.10
  60.8 67.2 all-gather.8
  130.3 37.9 all-gather.12
  222.6 121.7 reduce-scatter.17
  346.4 50.5 all-gather.16
  398.4 67.0 all-gather.14
  467.1 68.5 all-gather.20
  537.8 50.5 all-gather.18
  633.8 120.3 reduce-scatter.21
  756.4 121.8 reduce-scatter.19
  894.3 68.5 all-gather.22
  1097.6 121.8 reduce-scatter.23
  1223.1 57.3 reduce-scatter.35
  1284.9 54.3 reduce-scatter.33
  1343.3 168.9 all-reduce.3
  1515.7 55.1 reduce-scatter.31
  1575.4 103.6 reduce-scatter.27
  1683.5 104.3 reduce-scatter.29
  1792.3 61.2 reduce-scatter.25
where the time goes:
time: 1870 us; the launch traced here: 1860 us
  waiting for transfers between devices  1220 us (65%)
  matrix products  305 us (16%)
  other arithmetic  160 us (9%)
  local copies, waits for them, and re-layouts  80.6 us (4%)
  blocking collectives  74.8 us (4%)
    unnamed x23, waiting for transfers between devices  265 us
    reduce_scatter x1, waiting for transfers between devices, on_device(): lax.psum_scatter(jnp.einsum('sbc,cd->sbd', row_block, out_full, preferred...  121 us
    reduce_scatter x1, waiting for transfers between devices, on_device(): lax.psum_scatter(jnp.einsum('sbf,fd->sbd', row_block, down_full, preferre...  113 us
    reduce_scatter x1, waiting for transfers between devices, on_device(): lax.psum_scatter(down_weight_grad, 'dp', scatter_dimension=1, tiled=True)  109 us
    reduce_scatter x1, waiting for transfers between devices, on_device(): lax.psum_scatter(up_weight_grad, 'dp', scatter_dimension=0, tiled=True)  104 us
    reduce_scatter x1, waiting for transfers between devices, on_device(): lax.psum_scatter(jnp.einsum('sbf,df->sbd', row_block, up_back, preferred_...  103 us
    reduce_scatter x1, waiting for transfers between devices, on_device(): lax.psum_scatter(jnp.einsum('sbc,dc->sbd', row_block, qkv_back, preferred...  89.7 us
    all_gather x1, waiting for transfers between devices, on_device(): normed_all_two = lax.all_gather(normed_two, 'tensor', axis=0, tiled=True)  68.5 us
  transfers between devices with their start and end apart: 19, of which 15 were waited for; matrix products, arithmetic and copies ran while one was open for 18% of the time, Pallas kernels for 0%

commit v1 on v0

--- a/solution.py
+++ b/solution.py
@@ -6,6 +6,23 @@
 HD = 64
 epsilon = 1e-06
 masked_score = -1e30
+
+
+def joined_along(blocks, dim):
+    lengths = list(blocks.shape[1:])
+    lengths[dim] *= blocks.shape[0]
+    return jnp.moveaxis(blocks, 0, dim).reshape(lengths)
+
+
+def grow_blocks(x, axis):
+    peers, position = (lax.axis_size(axis), lax.axis_index(axis))
+    pieces, bit = (x[None], 1)
+    while bit < peers:
+        other = lax.ppermute(pieces, axis, [(i, i ^ bit) for i in range(peers)])
+        low = position & bit == 0
+        pieces = jnp.concatenate([jnp.where(low, pieces, other), jnp.where(low, other, pieces)])
+        bit *= 2
+    return pieces
 
 
 def layer_norm(values, gain, shift):
@@ -131,7 +148,7 @@
     )[:, :, None]
     input_float = inputs.astype(jnp.float32)
     normed_one = layer_norm(input_float, gain_one, shift_one).astype(jnp.bfloat16)
-    normed_all = lax.all_gather(normed_one, "tensor", axis=0, tiled=True)
+    normed_all = joined_along(grow_blocks(normed_one, "tensor"), 0)
     qkv_rows = (
         jnp.einsum("sbd,dc->sbc", normed_all, qkv_matrix, preferred_element_type=jnp.float32)
         + bias_row

time: 1870 us -> 1770 us (0.947)
  waiting for transfers between devices: 1220 us -> 1130 us
    unnamed x23 -> x21, waiting for transfers between devices: 265 us -> 79.3 us
    reduce_scatter x0 -> x1, waiting for transfers between devices: none -> 88.6 us  [on_device(): lax.psum_scatter(qkv_weight_grad, 'dp', scatter_dimension=0, tiled=True)]
    all_gather x1 -> x0, waiting for transfers between devices: 54.6 us -> none  [on_device(): normed_all = lax.all_gather(normed_one, 'tensor', axis=0, tiled=True)]
    ppermute x0 -> x1, waiting for transfers between devices: none -> 35.7 us  [grow_blocks(): other = lax.ppermute(pieces, axis, [(i, i ^ bit) for i in range(peers)])]
    reduce_scatter x1, waiting for transfers between devices: 89.7 us -> 113 us  [on_device(): lax.psum_scatter(jnp.einsum('sbc,dc->sbd', row_block, qkv_back, preferred...]
    unnamed x97 -> x92, local copies, waits for them, and re-layouts: 42 us -> 38.3 us
  transfers between devices with their start and end apart: 19 -> 19, of which waited for: 15 -> 15; matrix products, arithmetic and copies ran while one was open for 18% -> 19% of each run, Pallas kernels for 0% -> 0%
where the time goes in v1:
time: 1770 us
  waiting for transfers between devices  1130 us (64%)
  matrix products  308 us (17%)
  other arithmetic  164 us (9%)
  blocking collectives  74.9 us (4%)
  local copies, waits for them, and re-layouts  70.4 us (4%)
    reduce_scatter x1, waiting for transfers between devices, on_device(): lax.psum_scatter(jnp.einsum('sbc,cd->sbd', row_block, out_full, preferred...  119 us
    reduce_scatter x1, waiting for transfers between devices, on_device(): lax.psum_scatter(jnp.einsum('sbf,fd->sbd', row_block, down_full, preferre...  113 us
    reduce_scatter x1, waiting for transfers between devices, on_device(): lax.psum_scatter(jnp.einsum('sbc,dc->sbd', row_block, qkv_back, preferred...  113 us
    reduce_scatter x1, waiting for transfers between devices, on_device(): lax.psum_scatter(down_weight_grad, 'dp', scatter_dimension=1, tiled=True)  109 us
    reduce_scatter x1, waiting for transfers between devices, on_device(): lax.psum_scatter(up_weight_grad, 'dp', scatter_dimension=0, tiled=True)  104 us
    reduce_scatter x1, waiting for transfers between devices, on_device(): lax.psum_scatter(jnp.einsum('sbf,df->sbd', row_block, up_back, preferred_...  103 us
    reduce_scatter x1, waiting for transfers between devices, on_device(): lax.psum_scatter(qkv_weight_grad, 'dp', scatter_dimension=0, tiled=True)  88.6 us
    unnamed x21, waiting for transfers between devices  79.3 us
  transfers between devices with their start and end apart: 19, of which 15 were waited for; matrix products, arithmetic and copies ran while one was open for 19% of the time, Pallas kernels for 0%

profile of v1, /device:TPU:0, one launch (start us, length us, event | category | flops | bytes accessed | tf_op | source)
XLA Modules:
  0.0 1765.3 jit_solution(10803852053678043916)
XLA Ops:
  12.1 23.8 %all_gather.33 = bf16[6,1,512]{0,1,2:T(2,128)(2,1)S(1)} all-gather(bf16[6,1,32]{0,1,2:T(2,128)(2,1)S(1)} %copy.88), channel_id=1, replica_groups=mesh['dp'=16,'tensor'=2] {'dp'}, dimensions={2}, use_global_device_ids=true | all-gather | bytes 6528 | tf_op jit(solution)/shard_map/all_gather | solution.py:122
  36.0 4.4 all_gather.34
  50.3 18.3 %all_gather.36 = bf16[2,1,512]{1,0,2:T(2,128)(2,1)S(1)} all-gather(bf16[2,1,32]{1,0,2:T(2,128)(2,1)S(1)} %copy.93), channel_id=1, replica_groups=mesh['dp'=16,'tensor'=2] {'dp'}, dimensions={2}, use_global_device_ids=true | all-gather | bytes 2176 | tf_op jit(solution)/shard_map/all_gather | solution.py:120
  70.9 35.7 %collective-permute-done = bf16[1,320,4,1024]{3,1,2,0:T(8,128)(2,1)} collective-permute-done((bf16[1,320,4,1024]{3,1,2,0:T(8,128)(2,1)}, bf16[1,320,4,1024]{3,1,2,0:T(8,128)(2,1)}, u32[]{:S(2)}, u32[]{:S(2)}) %collective-permute-start) | collective-permute-done | bytes 2621472 | tf_op jit(solution)/shard_map/ppermute | solution.py:21
  117.1 14.0 fusion.50
  131.2 10.6 copy.94
  141.8 5.3 slice_bitcast_fusion
  147.1 51.8 %while.22 = (s32[]{:T(128)}, bf16[4,640,8,64]{1,3,2,0:T(8,128)(2,1)}, f32[4,8,640]{2,1,0:T(8,128)}, bf16[4,640,8,64]{1,3,2,0:T(8,128)(2,1)}, pred[4,640]{1,0:T(4...) while((s32[]{:T(128)}, ...), condition=%wide.region_5.6_spmd, body=%wide.region_2.5_spmd.sunk | while | flops 878504960 | bytes 42113112 | solution.py:161
  154.8 5.5 fusion.136
  167.6 5.5 fusion.136
  180.5 5.5 fusion.136
  193.3 5.5 fusion.136
  198.8 4.9 copy.95
  203.8 8.9 fusion.79
  213.5 118.7 %reduce-scatter.19.cloned.1.call-done = f32[320,4,1024]{2,0,1:T(8,128)} async-done(((f32[640,4,1024]{2,0,1:T(8,128)}), f32[320,4,1024]{2,0,1:T(8,128)}) %reduce-scatter.19.cloned.1.call-update) | async-done | bytes 5242896 | tf_op jit(solution)/shard_map/reduce_scatter | solution.py:164
  332.3 4.1 fusion.96
  341.0 7.3 fusion.75
  349.2 21.3 %all_gather.40 = bf16[1,2048]{1,0:T(2,128)(2,1)S(1)} all-gather(bf16[1,128]{1,0:T(2,128)(2,1)S(1)} %copy-done.29), channel_id=1, replica_groups=mesh['dp'=16,'tensor'=2] {'dp'}, dimensions={1}, use_global_device_ids=true | all-gather | bytes 4352 | tf_op jit(solution)/shard_map/all_gather | solution.py:121
  370.5 14.3 all-gather.14.cloned.1.call-done
  384.9 68.5 %all-gather.12.cloned.1.call-done = bf16[640,4,1024]{2,0,1:T(8,128)(2,1)} async-done(((bf16[320,4,1024]{2,0,1:T(8,128)(2,1)}), bf16[640,4,1024]{2,0,1:T(8,128)(2,1)}) %all-gather.12.cloned.1.call-update) | async-done | bytes 5242896 | tf_op jit(solution)/shard_map/all_gather | solution.py:172
  453.4 24.9 %fusion.66 = (u8[640,2048]{1,0:T(8,128)(4,1)S(1)}, u8[640,2048]{1,0:T(8,128)(4,1)S(1)}, f32[640,4,2048]{2,0,1:T(8,128)}) fusion(f32[2048]{0:T(1024)S(1)} %bitcast.244, bf16[640,4,1024]{2,0,1:T(8,128)(2,1)} %all-gather.12.cloned.1.call-done, bf16[1024,2048]{1,0:T(8,128)(2,1)} %all-gather.14.cloned.1.call-done), kind=kOutput, calls=%fused_computation.109 | convolution fusion | flops 10808197120 | bytes 33038336 | tf_op jit(solution)/shard_map/sbd,df->sbf/dot_general | solution.py:174
  478.2 51.1 %multiply_convert_fusion.1 = (bf16[640,4,2048]{2,0,1:T(8,128)(2,1)}, f32[640,4,2048]{2,0,1:T(8,128)}) fusion(f32[640,4,2048]{2,0,1:T(8,128)} %get-tuple-element.226, f32[2048]{0:T(1024)S(1)} %bitcast.245, u8[640,2048]{1,0:T(8,128)(4,1)S(1)} %get-tuple-element.154, u8[640,2048]{1,0:T(8,128)(4,1)S(1)} %get-tuple-element.153), kind=kLoop, calls=%fused_computation.64 | loop fusion | flops 372244480 | bytes 55058432 | tf_op jit(solution)/shard_map/convert_element_type | solution.py:177
  529.4 46.7 %all-gather.16.cloned.1.call-done = bf16[2048,1024]{0,1:T(8,128)(2,1)} async-done(((bf16[2048,64]{0,1:T(8,128)(2,1)}), bf16[2048,1024]{0,1:T(8,128)(2,1)}) %all-gather.16.cloned.1.call-update) | async-done | bytes 4194320 | tf_op jit(solution)/shard_map/all_gather | solution.py:119
  576.1 28.4 %convert_reduce_fusion = (f32[2048]{0:T(1024)}, bf16[640,4,2048]{2,0,1:T(8,128)(2,1)}) fusion(f32[640,4,2048]{2,0,1:T(8,128)} %get-tuple-element.198, bf16[640,4,1024]{2,0,1:T(8,128)(2,1)} %all-gather.18.cloned.1.call-done, bf16[2048,1024]{0,1:T(8,128)(2,1)} %all-gather.16.cloned.1.call-done, f32[640,4,2048]{2,0,1:T(8,128)} %get-tuple-element.226, ...), kind=kOutput, calls=%fused_computation.62 | convolution fusion | flops 10826545152 | bytes 61882368 | tf_op jit(solution)/shard_map/sbd,fd->sbf/dot_general | solution.py:194
  604.6 17.4 fusion.70
  622.0 17.5 fusion.68
  639.6 102.9 %reduce-scatter.23.cloned.1.call-done = f32[320,4,1024]{2,0,1:T(8,128)} async-done(((f32[640,4,1024]{2,0,1:T(8,128)}), f32[320,4,1024]{2,0,1:T(8,128)}) %reduce-scatter.23.cloned.1.call-update) | async-done | bytes 5242896 | tf_op jit(solution)/shard_map/reduce_scatter | solution.py:202
  742.5 6.0 fusion.92
  748.5 4.8 multiply_reduce_fusion.1
  753.2 113.4 %reduce-scatter.21.cloned.1.call-done = f32[320,4,1024]{2,0,1:T(8,128)} async-done(((f32[640,4,1024]{2,0,1:T(8,128)}), f32[320,4,1024]{2,0,1:T(8,128)}) %reduce-scatter.21.cloned.1.call-update) | async-done | bytes 5242896 | tf_op jit(solution)/shard_map/reduce_scatter | solution.py:179
  866.7 11.6 fusion.94
  882.8 68.5 %all-gather.20.cloned.1.call-done = bf16[640,4,1024]{2,0,1:T(8,128)(2,1)} async-done(((bf16[320,4,1024]{2,0,1:T(8,128)(2,1)}), bf16[640,4,1024]{2,0,1:T(8,128)(2,1)}) %all-gather.20.cloned.1.call-update) | async-done | bytes 5242896 | tf_op jit(solution)/shard_map/all_gather | solution.py:213
  951.2 7.2 convolution_convert_fusion
  958.4 113.2 %while.23 = (s32[]{:T(128)}, bf16[4,640,1536]{1,2,0:T(8,128)(2,1)}, bf16[4,640,8,64]{1,3,2,0:T(8,128)(2,1)S(1)}, pred[4,640]{1,0:T(4,128)(4,1)S(1)}, bf16[4,640,...) while((s32[]{:T(128)}, bf16[4,640,1536]{1,2,0:T(8,128)(2,1)}, ...), condition=%wide.region_15.16_spmd, body=%wide.region_13.15_spmd.sunk | while | flops 2134174720 | bytes 108898144 | solution.py:224
  959.2 4.5 subtract_exponential_fusion.3
  963.7 7.9 multiply_reduce_fusion.5
  971.6 5.9 multiply_convert_fusion.3
  987.5 4.5 subtract_exponential_fusion.3
  992.0 7.9 multiply_reduce_fusion.5
  999.8 5.9 multiply_convert_fusion.3
  1015.8 4.5 subtract_exponential_fusion.3
  1020.3 7.9 multiply_reduce_fusion.5
  1028.1 5.9 multiply_convert_fusion.3
  1044.1 4.5 subtract_exponential_fusion.3
  1048.6 7.9 multiply_reduce_fusion.5
  1056.4 5.9 multiply_convert_fusion.3
  1071.6 14.4 fusion.51
  1088.8 4.5 convert_reduce_fusion.1
  1095.0 113.1 %reduce-scatter.25.cloned.1.call-done = f32[320,4,1024]{2,0,1:T(8,128)} async-done(((f32[640,4,1024]{2,0,1:T(8,128)}), f32[320,4,1024]{2,0,1:T(8,128)}) %reduce-scatter.25.cloned.1.call-update) | async-done | bytes 5242896 | tf_op jit(solution)/shard_map/reduce_scatter | solution.py:237
  1208.1 4.3 fusion.93
  1216.1 7.1 all-reduce
  1228.9 17.6 convolution_bitcast_fusion.1
  1246.5 17.4 convolution_bitcast_fusion
  1264.2 7.7 fusion.82
  1271.9 14.0 convolution_bitcast_fusion.2
  1287.4 8.3 copy.101
  1295.7 31.6 %reduce-scatter.37.cloned.1.call-done = f32[32,2]{1,0:T(8,128)} async-done(((f32[512,2]{1,0:T(8,128)}), f32[32,2]{1,0:T(8,128)}) %reduce-scatter.37.cloned.1.call-update) | async-done | bytes 272
  1328.8 5.5 add_add_fusion.2
  1334.3 5.7 copy.102
  1340.0 45.5 %reduce-scatter.35.cloned.1.call-done = f32[32,6]{1,0:T(8,128)} async-done(((f32[512,6]{1,0:T(8,128)}), f32[32,6]{1,0:T(8,128)}) %reduce-scatter.35.cloned.1.call-update) | async-done | bytes 784
  1389.9 104.3 %reduce-scatter.31.cloned.1.call-done = f32[64,2048]{1,0:T(8,128)} async-done(((f32[1024,2048]{1,0:T(8,128)}), f32[64,2048]{1,0:T(8,128)}) %reduce-scatter.31.cloned.1.call-update) | async-done | bytes 524304 | tf_op jit(solution)/shard_map/reduce_scatter | solution.py:261
  1494.2 109.4 %reduce-scatter.33.cloned.1.call-done = f32[2048,64]{0,1:T(8,128)} async-done(((f32[2048,1024]{0,1:T(8,128)}), f32[2048,64]{0,1:T(8,128)}) %reduce-scatter.33.cloned.1.call-update) | async-done | bytes 524304 | tf_op jit(solution)/shard_map/reduce_scatter | solution.py:262
  1603.6 66.0 %reduce-scatter.29.cloned.1.call-done = f32[512,64]{0,1:T(8,128)} async-done(((f32[512,1024]{0,1:T(8,128)}), f32[512,64]{0,1:T(8,128)}) %reduce-scatter.29.cloned.1.call-update) | async-done | bytes 131088 | tf_op jit(solution)/shard_map/reduce_scatter | solution.py:260
  1669.5 88.6 %reduce-scatter.27.cloned.1.call-done = f32[64,3,512]{2,0,1:T(8,128)} async-done(((f32[1024,3,512]{2,0,1:T(8,128)}), f32[64,3,512]{2,0,1:T(8,128)}) %reduce-scatter.27.cloned.1.call-update) | async-done | bytes 393232 | tf_op jit(solution)/shard_map/reduce_scatter | solution.py:259
  (214 shorter events, 128.7 us)
Async XLA Ops:
  7.2 36.4 %copy-start.1 = (bf16[320,4,1024]{2,1,0:T(4,128)(2,1)S(1)}, bf16[320,4,1024]{2,1,0:T(4,128)(2,1)}, u32[]{:S(2)}) copy-start(bf16[320,4,1024]{2,1,0:T(4,128)(2,1)} %param.19) | copy-start | bytes 7864324
  7.2 106.7 %all-gather.8.cloned.1.call-start = ((), (), s32[]{:S(2)}) async-start(), calls=%async_computation.11 | async-start | bytes 3342336 | tf_op jit(solution)/shard_map/all_gather | solution.py:116
  7.9 195.9 %all-gather.10.cloned.1.call-start = ((), (), s32[]{:S(2)}) async-start(), calls=%async_computation.12 | async-start | bytes 1114112 | tf_op jit(solution)/shard_map/all_gather | solution.py:117
  40.4 9.9 copy-start.28
  40.4 30.5 %copy-start.26 = (s32[4,640]{1,0:T(4,128)S(1)}, s32[4,640]{1,0:T(4,128)}, u32[]{:S(2)}) copy-start(s32[4,640]{1,0:T(4,128)} %param.20) | copy-start | bytes 30724
  43.6 66.5 %copy-start.10 = (f32[320,4]{0,1:T(4,128)}, f32[320,4]{0,1:T(4,128)S(1)}, u32[]{:S(2)}) copy-start(f32[320,4]{0,1:T(4,128)S(1)} %broadcast_multiply_fusion.1) | copy-start | bytes 15364
  45.1 0.7 copy-start.17
  45.2 64.9 %copy-start.12 = (f32[320,4]{0,1:T(4,128)}, f32[320,4]{0,1:T(4,128)S(1)}, u32[]{:S(2)}) copy-start(f32[320,4]{0,1:T(4,128)S(1)} %fusion.90) | copy-start | bytes 15364
  45.8 64.3 %copy-start.14 = (f32[1,2,512]{2,0,1:T(1,128)}, f32[1,2,512]{2,0,1:T(1,128)S(1)}, u32[]{:S(2)}) copy-start(f32[1,2,512]{2,0,1:T(1,128)S(1)} %get-tuple-element.222) | copy-start | bytes 12292
  48.2 58.4 %collective-permute-start = (bf16[1,320,4,1024]{3,1,2,0:T(8,128)(2,1)}, bf16[1,320,4,1024]{3,1,2,0:T(8,128)(2,1)}, u32[]{:S(2)}, u32[]{:S(2)}) collective-permute-start(bf16[1,320,4,1024]{3,1,2,0:T(8,128)(2,1)} %fusion.76), channel_id=1, source_target_pairs={{0,1},{1,0},{2,3},{3,2},{4,5},{5,4},{6,7},{7,6},{8,9},{9,8},{10,11... | collective-permute-start | bytes 7864328 | tf_op jit(solution)/shard_map/ppermute | solution.py:21
  50.1 282.1 %reduce-scatter.19.cloned.1.call-start = ((), (), s32[]{:S(2)}) async-start(), calls=%async_computation.13 | async-start | bytes 15728640 | tf_op jit(solution)/shard_map/reduce_scatter | solution.py:164
  117.1 14.0 copy-start.9
  198.8 13.9 copy-start.7
  212.7 119.6 %copy-start.2 = (bf16[320,4,1024]{2,1,0:T(4,128)(2,1)S(1)}, bf16[320,4,1024]{2,1,0:T(4,128)(2,1)}, u32[]{:S(2)}) copy-start(bf16[320,4,1024]{2,1,0:T(4,128)(2,1)} %param.19) | copy-start | bytes 7864324
  212.7 119.6 %copy-start.22 = (f32[1,2,512]{2,0,1:T(1,128)S(1)}, f32[1,2,512]{2,0,1:T(1,128)}, u32[]{:S(2)}) copy-start(f32[1,2,512]{2,0,1:T(1,128)} %get-tuple-element.221) | copy-start | bytes 12292
  212.7 172.1 %all-gather.14.cloned.1.call-start = ((), (), s32[]{:S(2)}) async-start(), calls=%async_computation.15 | async-start | bytes 4456448 | tf_op jit(solution)/shard_map/all_gather | solution.py:118
  213.3 240.1 %all-gather.12.cloned.1.call-start = ((), (), s32[]{:S(2)}) async-start(), calls=%async_computation.14 | async-start | bytes 7864320 | tf_op jit(solution)/shard_map/all_gather | solution.py:172
  336.4 2.4 copy-start
  336.4 2.4 copy-start.16
  336.4 2.3 copy-start.19
  340.9 188.5 %all-gather.18.cloned.1.call-start = ((), (), s32[]{:S(2)}) async-start(), calls=%async_computation.18 | async-start | bytes 7864320 | tf_op jit(solution)/shard_map/all_gather | solution.py:190
  341.0 8.2 copy-start.29
  348.4 227.7 %all-gather.16.cloned.1.call-start = ((), (), s32[]{:S(2)}) async-start(), calls=%async_computation.16 | async-start | bytes 4456448 | tf_op jit(solution)/shard_map/all_gather | solution.py:119
  349.1 393.3 %reduce-scatter.23.cloned.1.call-start = ((), (), s32[]{:S(2)}) async-start(), calls=%async_computation.19 | async-start | bytes 15728640 | tf_op jit(solution)/shard_map/reduce_scatter | solution.py:202
  622.0 244.7 %reduce-scatter.21.cloned.1.call-start = ((), (), s32[]{:S(2)}) async-start(), calls=%async_computation.17 | async-start | bytes 15728640 | tf_op jit(solution)/shard_map/reduce_scatter | solution.py:179
  639.5 311.7 %all-gather.20.cloned.1.call-start = ((), (), s32[]{:S(2)}) async-start(), calls=%async_computation.20 | async-start | bytes 7864320 | tf_op jit(solution)/shard_map/all_gather | solution.py:213
  742.5 6.0 copy-start.4
  748.5 118.2 %copy-start.21 = (f32[1,2,512]{2,0,1:T(1,128)S(1)}, f32[1,2,512]{2,0,1:T(1,128)}, u32[]{:S(2)}) copy-start(f32[1,2,512]{2,0,1:T(1,128)} %get-tuple-element.218) | copy-start | bytes 12292
  878.3 2.3 copy-start.6
  882.5 325.6 %reduce-scatter.25.cloned.1.call-start = ((), (), s32[]{:S(2)}) async-start(), calls=%async_computation.21 | async-start | bytes 15728640 | tf_op jit(solution)/shard_map/reduce_scatter | solution.py:237
  882.8 75.7 %copy-start.8 = (bf16[4,640,8,64]{1,3,2,0:T(8,128)(2,1)S(1)}, bf16[4,640,8,64]{1,3,2,0:T(8,128)(2,1)}, u32[]{:S(2)}) copy-start(bf16[4,640,8,64]{1,3,2,0:T(8,128)(2,1)} %copy-done.7) | copy-start | bytes 7864324
  1086.0 0.7 copy-start.30
  1086.0 1.2 copy-start.27
  1086.0 2.7 copy-start.25
  1086.0 2.7 copy-start.20
  1086.0 2.7 copy-start.23
  1086.0 2.7 copy-start.24
  1086.1 199.9 %reduce-scatter.39.cloned.1.call-start = ((), (), s32[]{:S(2)}) async-start(), calls=%async_computation.28 | async-start | bytes 1114112
  1088.6 119.5 %copy-start.3 = (bf16[320,4,1024]{2,1,0:T(4,128)(2,1)S(1)}, bf16[320,4,1024]{2,1,0:T(4,128)(2,1)}, u32[]{:S(2)}) copy-start(bf16[320,4,1024]{2,1,0:T(4,128)(2,1)} %param.19) | copy-start | bytes 7864324
  1088.6 119.5 %copy-start.11 = (f32[320,4]{0,1:T(4,128)S(1)}, f32[320,4]{0,1:T(4,128)}, u32[]{:S(2)}) copy-start(f32[320,4]{0,1:T(4,128)} %copy-done.10) | copy-start | bytes 15364
  1088.6 119.5 %copy-start.15 = (f32[1,2,512]{2,0,1:T(1,128)S(1)}, f32[1,2,512]{2,0,1:T(1,128)}, u32[]{:S(2)}) copy-start(f32[1,2,512]{2,0,1:T(1,128)} %copy-done.14) | copy-start | bytes 12292
  1088.6 238.7 %reduce-scatter.37.cloned.1.call-start = ((), (), s32[]{:S(2)}) async-start(), calls=%async_computation.27 | async-start | bytes 278528
  1093.3 119.1 %copy-start.18 = (f32[320,4]{0,1:T(4,128)S(1)}, f32[320,4]{0,1:T(4,128)}, u32[]{:S(2)}) copy-start(f32[320,4]{0,1:T(4,128)} %copy-done.17) | copy-start | bytes 15364
  1093.3 119.2 %copy-start.13 = (f32[320,4]{0,1:T(4,128)S(1)}, f32[320,4]{0,1:T(4,128)}, u32[]{:S(2)}) copy-start(f32[320,4]{0,1:T(4,128)} %copy-done.12) | copy-start | bytes 15364
  1095.0 290.5 %reduce-scatter.35.cloned.1.call-start = ((), (), s32[]{:S(2)}) async-start(), calls=%async_computation.26 | async-start | bytes 278528
  1208.1 4.4 copy-start.5
  1228.8 265.4 %reduce-scatter.31.cloned.1.call-start = ((), (), s32[]{:S(2)}) async-start(), calls=%async_computation.24 | async-start | bytes 8912896 | tf_op jit(solution)/shard_map/reduce_scatter | solution.py:261
  1246.4 357.1 %reduce-scatter.33.cloned.1.call-start = ((), (), s32[]{:S(2)}) async-start(), calls=%async_computation.25 | async-start | bytes 8912896 | tf_op jit(solution)/shard_map/reduce_scatter | solution.py:262
  1263.9 405.7 %reduce-scatter.29.cloned.1.call-start = ((), (), s32[]{:S(2)}) async-start(), calls=%async_computation.23 | async-start | bytes 2228224 | tf_op jit(solution)/shard_map/reduce_scatter | solution.py:260
  1271.9 486.2 %reduce-scatter.27.cloned.1.call-start = ((), (), s32[]{:S(2)}) async-start(), calls=%async_computation.22 | async-start | bytes 6684672 | tf_op jit(solution)/shard_map/reduce_scatter | solution.py:259
Sparse Core Ops, SparseCore 0:
  10.2 49.1 all-gather.7
  61.6 36.5 all-gather.9
  212.9 119.3 reduce-scatter.18
  334.3 50.5 all-gather.13
  386.3 67.0 all-gather.11
  454.8 68.5 all-gather.17
  525.5 50.5 all-gather.15
  622.1 120.3 reduce-scatter.22
  744.8 121.8 reduce-scatter.20
  882.6 68.5 all-gather.19
  1086.2 121.8 reduce-scatter.24
  1211.6 57.4 reduce-scatter.38
  1273.0 54.2 reduce-scatter.36
  1331.1 54.3 reduce-scatter.34
  1390.5 103.5 reduce-scatter.30
  1499.2 104.3 reduce-scatter.32
  1608.2 61.3 reduce-scatter.28
  1673.9 84.1 reduce-scatter.26
